TPU v7x, 512 devices: a whole 4x4x16 slice. The times are simulated.
512 devices in a mesh: blk: 32 (over x, z_lo), expert: 16 (over z_hi, y, core).
Axes of the slice: x: 4, y: 4, z: 16 (z_hi: 2, z_lo: 8; z = z_hi * 8 + z_lo), core: 2. Of those that a mesh axis runs over, the one named last changes fastest.
Arguments:
- short_draft: bfloat16 [1024, 64, 3, 512], P(('blk', 'expert')), may hold values from -42 to 42
- short_mask: int32 [1024, 64, 64], P(('blk', 'expert')), may hold values from 0 to 1, as said below
- short_keys: bfloat16 [1024, 128, 512], P(('blk', 'expert')), may hold values from -16 to 16
- short_values: bfloat16 [1024, 128, 512], P(('blk', 'expert')), may hold values from -6 to 6
- short_length: int32 [1024], P(('blk', 'expert')), may hold values from 1 to 128, 65536 in all
- short_x: bfloat16 [65536, 1024], P(('blk', 'expert')), may hold values from -44 to 44
- accepted: int32 [1024, 8], P(('blk', 'expert')), may hold values from 0 to 63, as said below
- long_draft: bfloat16 [32, 64, 3, 512], P('expert'), may hold values from -42 to 42
- long_mask: int32 [32, 64, 64], P('expert'), may hold values from 0 to 1, as said below
- long_keys: bfloat16 [32, 8192, 512], P('expert', 'blk'), may hold values from -15 to 15
- long_values: bfloat16 [32, 8192, 512], P('expert', 'blk'), may hold values from -6 to 6
- long_x: bfloat16 [32, 64, 1024], P('expert', 'blk'), may hold values from -44 to 44
- out_weight: bfloat16 [512, 1024], P('expert'), may hold values from -0.25 to 0.25
- norm_gain: bfloat16 [1024], replicated, may hold values from 0.099609375 to 1.8984375
- router: bfloat16 [1024, 16], replicated, may hold values from -0.1875 to 0.1875
- route_ids: int32 [67584, 2], P(('blk', 'expert')), may hold values from 0 to 15, all different within a row; in each aligned block of 132 rows (0 to 131, 132 to 263, ...) at most 21 rows name the same one
- expert_in: bfloat16 [16, 1408, 2, 1024], P('expert', 'blk'), may hold values from -0.1875 to 0.1875
- expert_out: bfloat16 [16, 1408, 1024], P('expert', 'blk'), may hold values from -0.15625 to 0.15625
Outputs:
- short_out: bfloat16 [65536, 1024], P(('blk', 'expert'))
- accepted_out: bfloat16 [1024, 8, 1024], P(('blk', 'expert'))
- long_out: bfloat16 [32, 64, 1024], P('expert', 'blk')
Inputs may be any that keep to these rules, and one draw needn't show every extreme that they name: short_mask[r, i, j] is 1 exactly when tree node j is node i or one of its ancestors; every node but the root 0 has a parent of smaller index. long_mask[r, i, j] is 1 exactly when tree node j is node i or one of its ancestors; every node but the root 0 has a parent of smaller index. accepted[r] lists 8 nodes of request r's tree, the root first and node 63 last, each the parent of the next. `route_ids`: a row's two experts differ; among the rows of one device no expert is named more than 21 times.
All inputs are finite; a program needn't handle non-finite values. No bound on the sum of `short_length` on one device may be relied on, other than what follows from the above.
Results may differ from a plain program's by a relative error of at most 0.011.
Values may be sent and summed in bfloat16 or wider, within the bound.
A program may use at most 64 MiB of HBM per device.

v0:
```python
import jax
import jax.numpy as jnp
from jax import lax
from jax.sharding import PartitionSpec as P

HEADS = 8
HD = 64


def combined_all(part, axis, combine):
    gathered = jax.tree.map(lambda a: lax.all_gather(a, axis), part)

    def take(source):
        return jax.tree.map(lambda a: lax.dynamic_index_in_dim(a, source, 0, False), gathered)

    return lax.fori_loop(
        1, lax.axis_size(axis), lambda source, state: combine(state, take(source)), take(0)
    )


def heads_of(tensor):
    return tensor.reshape(tensor.shape[:-1] + (HEADS, HD))


def block_part(queries, keyside, values, allowed):
    head_size = queries.shape[-1]
    scores = jnp.einsum(
        "rqhe,rkhe->rqhk", queries, keyside, preferred_element_type=jnp.float32
    ) * head_size ** (-0.5)
    scores = jnp.where(allowed[:, :, None, :], scores, -jnp.inf)
    peaks = jnp.max(scores, axis=-1)
    weights = jnp.exp(scores - peaks[..., None]).astype(jnp.bfloat16)
    totals = jnp.sum(weights.astype(jnp.float32), axis=-1)
    output = jnp.einsum("rqhk,rkhe->rqhe", weights, values, preferred_element_type=jnp.float32)
    return (peaks, totals, output.reshape(output.shape[0], output.shape[1], -1))


def expand(factor, output):
    shaped = output.reshape(factor.shape + (-1,))
    return (shaped * factor[..., None]).reshape(output.shape)


def divide(output, totals):
    shaped = output.reshape(totals.shape + (-1,))
    return (shaped / totals[..., None]).reshape(output.shape)


def pair_join(former, latter):
    highest = jnp.maximum(former[0], latter[0])
    former_scale = jnp.exp(former[0] - highest)
    latter_scale = jnp.exp(latter[0] - highest)
    totals = former_scale * former[1] + latter_scale * latter[1]
    output = expand(former_scale, former[2]) + expand(latter_scale, latter[2])
    return (highest, totals, output)


def finish(joined):
    return divide(joined[2], joined[1]).astype(jnp.bfloat16)


def on_device(
    short_draft,
    short_mask,
    short_keys,
    short_values,
    short_length,
    short_x,
    accepted,
    long_draft,
    long_mask,
    long_keys,
    long_values,
    long_x,
    out_weight,
    norm_gain,
    router,
    route_ids,
    expert_in,
    expert_out,
):
    short_count = short_draft.shape[0]
    tree_size = short_draft.shape[1]
    cache_size = short_keys.shape[1]
    model_width = out_weight.shape[1]
    short_queries = heads_of(short_draft[:, :, 0])
    visible = jnp.broadcast_to(
        jnp.arange(cache_size)[None, None, :] < short_length[:, None, None],
        (short_count, tree_size, cache_size),
    )
    short_cache = block_part(short_queries, heads_of(short_keys), heads_of(short_values), visible)
    short_tree = block_part(
        short_queries,
        heads_of(short_draft[:, :, 1]),
        heads_of(short_draft[:, :, 2]),
        short_mask == 1,
    )
    short_attn = finish(pair_join(short_cache, short_tree))
    long_count = long_keys.shape[0]
    cache_local = long_keys.shape[1]
    long_queries = heads_of(long_draft[:, :, 0])
    everything = jnp.ones((long_count, tree_size, cache_local), dtype=bool)
    local_part = block_part(long_queries, heads_of(long_keys), heads_of(long_values), everything)
    share_rows = tree_size // lax.axis_size("blk")
    share_start = lax.axis_index("blk") * share_rows
    merged = combined_all(local_part, "blk", pair_join)
    cache_part = tuple(
        (lax.dynamic_slice_in_dim(member, share_start, share_rows, 1) for member in merged)
    )
    share_queries = lax.dynamic_slice_in_dim(long_queries, share_start, share_rows, 1)
    share_mask = lax.dynamic_slice_in_dim(long_mask, share_start, share_rows, 1)
    long_tree = block_part(
        share_queries, heads_of(long_draft[:, :, 1]), heads_of(long_draft[:, :, 2]), share_mask == 1
    )
    long_attn = finish(pair_join(cache_part, long_tree))
    attn_rows = jnp.concatenate(
        [short_attn.reshape(-1, short_attn.shape[-1]), long_attn.reshape(-1, long_attn.shape[-1])],
        axis=0,
    )
    residual = jnp.concatenate([short_x, long_x.reshape(-1, model_width)], axis=0)
    row_count = attn_rows.shape[0]
    projected = jnp.dot(
        attn_rows,
        lax.all_gather(out_weight, "expert", axis=0, tiled=True),
        preferred_element_type=jnp.float32,
    )
    layer_state = (residual.astype(jnp.float32) + projected).astype(jnp.bfloat16)
    state_wide = layer_state.astype(jnp.float32)
    normed = (
        state_wide
        * lax.rsqrt(jnp.mean(state_wide * state_wide, axis=-1, keepdims=True) + 1e-06)
        * norm_gain.astype(jnp.float32)
    ).astype(jnp.bfloat16)
    gate_probs = jax.nn.sigmoid(jnp.dot(normed, router, preferred_element_type=jnp.float32))
    expert_count = router.shape[1]
    capacity = (row_count * 10 + 4 * expert_count - 1) // (4 * expert_count)
    one_hot = route_ids[:, :, None] == jnp.arange(expert_count, dtype=jnp.int32)[None, None, :]
    gate_pick = jnp.sum(jnp.where(one_hot, gate_probs[:, None, :], 0.0), axis=-1)
    flat_hot = one_hot.reshape(2 * row_count, expert_count).astype(jnp.int32)
    earlier = jnp.cumsum(flat_hot, axis=0) - flat_hot
    slot_in = jnp.sum(earlier * flat_hot, axis=-1)
    target = route_ids.reshape(-1) * capacity + slot_in
    placement = (
        jnp.arange(expert_count * capacity, dtype=jnp.int32)[:, None] == target[None, :]
    ).astype(jnp.bfloat16)
    dispatch = jnp.dot(
        placement, jnp.repeat(normed, 2, axis=0), preferred_element_type=jnp.float32
    ).astype(jnp.bfloat16)
    dispatch = dispatch.reshape(expert_count, capacity, model_width)
    received = lax.all_to_all(dispatch, "expert", split_axis=0, concat_axis=0, tiled=True)
    flat_rows = received.reshape(-1, model_width)
    weight_in = lax.all_gather(expert_in, "blk", axis=1, tiled=True)[0]
    weight_out = lax.all_gather(expert_out, "blk", axis=1, tiled=True)[0]
    gate_part = jnp.einsum(
        "rd,nd->rn", flat_rows, weight_in[:, 0, :], preferred_element_type=jnp.float32
    )
    up_part = jnp.einsum(
        "rd,nd->rn", flat_rows, weight_in[:, 1, :], preferred_element_type=jnp.float32
    )
    inner_act = (jax.nn.gelu(gate_part, approximate=True) * up_part).astype(jnp.bfloat16)
    expert_sum = jnp.dot(inner_act, weight_out, preferred_element_type=jnp.float32)
    expert_y = expert_sum.astype(jnp.bfloat16).reshape(expert_count, capacity, model_width)
    returned = lax.all_to_all(expert_y, "expert", split_axis=0, concat_axis=0, tiled=True)
    per_route = jnp.einsum(
        "sa,sd->ad",
        placement,
        returned.reshape(-1, model_width),
        preferred_element_type=jnp.float32,
    )
    moe_sum = jnp.sum(per_route.reshape(row_count, 2, model_width) * gate_pick[:, :, None], axis=1)
    layer_out = (state_wide + moe_sum).astype(jnp.bfloat16)
    short_total = short_x.shape[0]
    short_out = layer_out[:short_total]
    long_out = layer_out[short_total:].reshape(long_x.shape)
    accepted_out = jnp.take_along_axis(
        short_out.reshape(short_count, tree_size, model_width), accepted[:, :, None], axis=1
    )
    return (short_out, accepted_out, long_out)


def solution(mesh):
    return jax.shard_map(
        on_device,
        mesh=mesh,
        in_specs=(
            P(("blk", "expert"), None, None, None),
            P(("blk", "expert"), None, None),
            P(("blk", "expert"), None, None),
            P(("blk", "expert"), None, None),
            P(("blk", "expert")),
            P(("blk", "expert"), None),
            P(("blk", "expert"), None),
            P("expert", None, None, None),
            P("expert", None, None),
            P("expert", "blk", None),
            P("expert", "blk", None),
            P("expert", "blk", None),
            P("expert", None),
            P(),
            P(),
            P(("blk", "expert"), None),
            P("expert", "blk", None, None),
            P("expert", "blk", None),
        ),
        out_specs=(
            P(("blk", "expert"), None),
            P(("blk", "expert"), None, None),
            P("expert", "blk", None),
        ),
        check_vma=False,
    )
```

profile of v0, /device:TPU:1, one launch (start us, length us, event | category | flops | bytes accessed | tf_op | source)
XLA Modules:
  0.0 905.2 jit_solution(18083236764553195508)
XLA Ops:
  7.2 1.1 fusion.65
  8.5 1.2 copy.132
  14.8 119.0 %all-gather = f32[64,64,8]{1,2,0:T(8,128)S(1)} all-gather(f32[2,64,8]{1,2,0:T(8,128)S(1)} %get-tuple-element.216), channel_id=2, replica_groups=mesh['blk'=32,'expert'=16] {'blk'}, dimensions={0}, use_global_device_ids=true | all-gather | bytes 135168 | tf_op jit(solution)/shard_map/all_gather | solution.py:11
  133.8 103.8 %all-gather.1 = f32[64,64,8]{1,2,0:T(8,128)S(1)} all-gather(f32[2,64,8]{1,2,0:T(8,128)S(1)} %convert_reduce_fusion), channel_id=3, replica_groups=mesh['blk'=32,'expert'=16] {'blk'}, dimensions={0}, use_global_device_ids=true | all-gather | bytes 135168 | tf_op jit(solution)/shard_map/all_gather | solution.py:11
  244.4 9.7 %all-gather.7.cloned.1.call-done = f32[32,2,64,512]{3,2,1,0:T(8,128)} async-done(((f32[1,2,64,512]{3,2,1,0:T(8,128)}), f32[32,2,64,512]{3,2,1,0:T(8,128)}) %all-gather.7.cloned.1.call-update) | async-done | bytes 8388624 | tf_op jit(solution)/shard_map/all_gather | solution.py:11
  255.1 62.8 %while.19 = (s32[]{:T(128)}, f32[2,64,8]{1,2,0:T(8,128)S(1)}, f32[2,64,8]{1,2,0:T(8,128)S(1)}, f32[2,64,512]{2,1,0:T(8,128)S(1)}, f32[32,2,64,8]{2,3,1,0:T(8,128...) while((s32[]{:T(128)}, f32[2,64,8]{1,2,0:T(8,128)S(1)}, ...), condition=%wide.region_7.8_spmd, body=%wide.region_6.7_spmd.sunk | while | flops 202757 | bytes 2941079 | solution.py:16
  256.0 1.1 fusion.84
  258.0 1.1 fusion.84
  260.1 1.1 fusion.84
  262.1 1.1 fusion.84
  264.1 1.1 fusion.84
  266.1 1.1 fusion.84
  268.2 1.1 fusion.84
  270.2 1.1 fusion.84
  272.2 1.1 fusion.84
  274.2 1.1 fusion.84
  276.3 1.1 fusion.84
  278.3 1.1 fusion.84
  280.3 1.1 fusion.84
  282.3 1.1 fusion.84
  284.4 1.1 fusion.84
  286.4 1.1 fusion.84
  288.4 1.1 fusion.84
  290.4 1.1 fusion.84
  292.5 1.1 fusion.84
  294.5 1.1 fusion.84
  296.5 1.1 fusion.84
  298.5 1.1 fusion.84
  300.6 1.1 fusion.84
  302.6 1.1 fusion.84
  304.6 1.1 fusion.84
  306.6 1.1 fusion.84
  308.7 1.1 fusion.84
  310.7 1.1 fusion.84
  312.7 1.1 fusion.84
  316.8 1.1 fusion.84
  318.8 32.4 %all-gather.9.cloned.1.call-done = bf16[512,1024]{1,0:T(8,128)(2,1)} async-done(((bf16[32,1024]{1,0:T(8,128)(2,1)}), bf16[512,1024]{1,0:T(8,128)(2,1)}) %all-gather.9.cloned.1.call-update) | async-done | bytes 1048592 | tf_op jit(solution)/shard_map/all_gather | solution.py:123
  351.2 1.7 multiply_reduce_fusion
  354.1 1.1 reshape.235
  355.2 4.0 all-to-all-start
  359.1 228.4 %all-gather.11.cloned.1.call-done = bf16[1,1408,2,1024]{3,2,0,1:T(2,128)(2,1)} async-done(((bf16[1,44,2,1024]{3,2,0,1:T(2,128)(2,1)}), bf16[1,1408,2,1024]{3,2,0,1:T(2,128)(2,1)}) %all-gather.11.cloned.1.call-update) | async-done | bytes 5767184 | tf_op jit(solution)/shard_map/all_gather | solution.py:151
  587.5 6.9 copy.188
  594.7 4.7 fusion.14
  599.4 228.0 %all-gather.13.cloned.1.call-done = bf16[1,1408,1024]{2,0,1:T(2,128)(2,1)} async-done(((bf16[1,44,1024]{2,0,1:T(2,128)(2,1)}), bf16[1,1408,1024]{2,0,1:T(2,128)(2,1)}) %all-gather.13.cloned.1.call-update) | async-done | bytes 2883600 | tf_op jit(solution)/shard_map/all_gather | solution.py:152
  827.4 6.6 fusion.16
  834.0 1.1 reshape.237
  835.1 33.9 %all-to-all-start.1 = ((bf16[16,21,1024]{2,1,0:T(8,128)(2,1)}), bf16[16,21,1024]{2,1,0:T(8,128)(2,1)S(1)}, u32[]{:S(2)}, u32[]{:S(2)}) async-start(bf16[16,21,1024]{2,1,0:T(8,128)(2,1)} %reshape.237), calls=%async_computation.1 | async-start | bytes 1572864 | tf_op jit(solution)/shard_map/all_to_all | solution.py:162
  869.7 26.1 %all-to-all-done.1 = bf16[16,21,1024]{2,1,0:T(8,128)(2,1)S(1)} async-done(((bf16[16,21,1024]{2,1,0:T(8,128)(2,1)}), bf16[16,21,1024]{2,1,0:T(8,128)(2,1)S(1)}, u32[]{:S(2)}, u32[]{:S(2)}) %all-to-all-start.1) | async-done | bytes 688160 | tf_op jit(solution)/shard_map/all_to_all | solution.py:162
  (335 shorter events, 46.7 us)
Async XLA Ops:
  7.2 862.3 %copy-start = (bf16[1024,16]{0,1:T(8,128)(2,1)S(1)}, bf16[1024,16]{0,1:T(8,128)(2,1)}, u32[]{:S(2)}) copy-start(bf16[1024,16]{0,1:T(8,128)(2,1)} %param.34) | copy-start | bytes 98308
  7.2 2.6 copy-start.2
  7.2 246.9 %all-gather.7.cloned.1.call-start = ((), (), s32[]{:S(2)}) async-start(), calls=%async_computation.2 | async-start | bytes 8650752 | tf_op jit(solution)/shard_map/all_gather | solution.py:11
  10.4 3.1 copy-start.7
  12.0 226.0 %copy-start.3 = (bf16[2,64,3,512]{3,1,2,0:T(8,128)(2,1)S(1)}, bf16[2,64,3,512]{3,1,2,0:T(8,128)(2,1)}, u32[]{:S(2)}) copy-start(bf16[2,64,3,512]{3,1,2,0:T(8,128)(2,1)} %param.20) | copy-start | bytes 1179652
  12.0 339.2 %all-gather.9.cloned.1.call-start = ((), (), s32[]{:S(2)}) async-start(), calls=%async_computation.3 | async-start | bytes 1114112 | tf_op jit(solution)/shard_map/all_gather | solution.py:123
  12.7 574.8 %all-gather.11.cloned.1.call-start = ((), (), s32[]{:S(2)}) async-start(), calls=%async_computation.4 | async-start | bytes 5947392 | tf_op jit(solution)/shard_map/all_gather | solution.py:151
  13.5 813.9 %all-gather.13.cloned.1.call-start = ((), (), s32[]{:S(2)}) async-start(), calls=%async_computation.5 | async-start | bytes 5947392 | tf_op jit(solution)/shard_map/all_gather | solution.py:152
  14.7 223.7 %copy-start.8 = (s32[2,64,64]{2,1,0:T(8,128)S(1)}, s32[2,64,64]{2,1,0:T(8,128)}, u32[]{:S(2)}) copy-start(s32[2,64,64]{2,1,0:T(8,128)} %param.21) | copy-start | bytes 98308
  14.8 223.8 %copy-start.5 = (bf16[2,128,512]{2,1,0:T(8,128)(2,1)S(1)}, bf16[2,128,512]{2,1,0:T(8,128)(2,1)}, u32[]{:S(2)}) copy-start(bf16[2,128,512]{2,1,0:T(8,128)(2,1)} %param.22) | copy-start | bytes 786436
  133.8 105.0 %copy-start.13 = (s32[2]{0:T(128)S(1)}, s32[2]{0:T(128)}, u32[]{:S(2)}) copy-start(s32[2]{0:T(128)} %param.24) | copy-start | bytes 28
  133.8 105.2 %copy-start.6 = (bf16[2,128,512]{2,1,0:T(8,128)(2,1)S(1)}, bf16[2,128,512]{2,1,0:T(8,128)(2,1)}, u32[]{:S(2)}) copy-start(bf16[2,128,512]{2,1,0:T(8,128)(2,1)} %param.23) | copy-start | bytes 786436
  240.7 0.9 copy-start.10
  240.7 0.9 copy-start.11
  240.7 0.9 copy-start.9
  255.1 96.1 %copy-start.4 = (bf16[128,1024]{1,0:T(8,128)(2,1)S(1)}, bf16[128,1024]{1,0:T(8,128)(2,1)}, u32[]{:S(2)}) copy-start(bf16[128,1024]{1,0:T(8,128)(2,1)} %param.25) | copy-start | bytes 786436
  355.2 239.3 %all-to-all-start = ((bf16[16,21,1024]{2,1,0:T(8,128)(2,1)}), bf16[16,21,1024]{2,1,0:T(8,128)(2,1)S(1)}, u32[]{:S(2)}, u32[]{:S(2)}) async-start(bf16[16,21,1024]{2,1,0:T(8,128)(2,1)} %reshape.235), calls=%async_computation | async-start | bytes 1572864 | tf_op jit(solution)/shard_map/all_to_all | solution.py:149
  834.0 35.3 %copy-start.12 = (s32[2,8]{1,0:T(2,128)S(1)}, s32[2,8]{1,0:T(2,128)}, u32[]{:S(2)}) copy-start(s32[2,8]{1,0:T(2,128)} %param.26) | copy-start | bytes 196
  835.1 60.6 %all-to-all-start.1 = ((bf16[16,21,1024]{2,1,0:T(8,128)(2,1)}), bf16[16,21,1024]{2,1,0:T(8,128)(2,1)S(1)}, u32[]{:S(2)}, u32[]{:S(2)}) async-start(bf16[16,21,1024]{2,1,0:T(8,128)(2,1)} %reshape.237), calls=%async_computation.1 | async-start | bytes 1572864 | tf_op jit(solution)/shard_map/all_to_all | solution.py:162
  896.6 2.1 copy-start.1
Sparse Core Ops, SparseCore 0:
  12.1 241.9 all-gather.6
  257.4 93.7 all-gather.8
  353.3 234.1 all-gather.10
  589.4 237.8 all-gather.12
where the time goes:
time: 907 us; the launch traced here: 905 us
  waiting for transfers between devices  526 us (58%)
  blocking collectives  223 us (25%)
  local copies, waits for them, and re-layouts  46.9 us (5%)
  other arithmetic  38.4 us (4%)
  starting transfers between devices  38 us (4%)
  matrix products  16.9 us (2%)
  between operations  14.3 us (2%)
    all_gather x1, waiting for transfers between devices, on_device(): weight_in = lax.all_gather(expert_in, 'blk', axis=1, tiled=True)[0]  228 us
    all_gather x1, waiting for transfers between devices, on_device(): weight_out = lax.all_gather(expert_out, 'blk', axis=1, tiled=True)[0]  228 us
    all_gather x2, blocking collectives, combined_all(): gathered = jax.tree.map(lambda a: lax.all_gather(a, axis), part)  223 us
    all_to_all x1, starting transfers between devices, on_device(): lax.all_to_all(expert_y, 'expert', split_axis=0, concat_axis=0, tiled=True)  33.9 us
    add x31, other arithmetic, pair_join(): output = expand(former_scale, former[2]) + expand(latter_scale, latter[2])  33.7 us
    all_gather x1, waiting for transfers between devices, on_device(): lax.all_gather(out_weight, 'expert', axis=0, tiled=True)  32.4 us
    all_to_all x1, waiting for transfers between devices, on_device(): lax.all_to_all(expert_y, 'expert', split_axis=0, concat_axis=0, tiled=True)  26.1 us
    mul x127, local copies, waits for them, and re-layouts, expand(): return (shaped * factor[..., None]).reshape(output.shape)  21.2 us
  transfers between devices with their start and end apart: 6, of which 5 were waited for; matrix products, arithmetic and copies ran while one was open for 10% of the time, Pallas kernels for 0%

commit v1 on v0

--- a/solution.py
+++ b/solution.py
@@ -149,7 +149,13 @@
     received = lax.all_to_all(dispatch, "expert", split_axis=0, concat_axis=0, tiled=True)
     flat_rows = received.reshape(-1, model_width)
     weight_in = lax.all_gather(expert_in, "blk", axis=1, tiled=True)[0]
-    weight_out = lax.all_gather(expert_out, "blk", axis=1, tiled=True)[0]
+    end_the_slots = lambda load, link_axis, in_dim: jnp.concatenate(
+        lax.all_to_all(
+            jnp.stack([load for _ in range(lax.axis_size(link_axis))], axis=0), link_axis, 0, 0
+        ),
+        axis=in_dim,
+    )
+    weight_out = end_the_slots(expert_out, "blk", 1)[0]
     gate_part = jnp.einsum(
         "rd,nd->rn", flat_rows, weight_in[:, 0, :], preferred_element_type=jnp.float32
     )

time: 907 us -> 787 us (0.87)
  waiting for transfers between devices: 526 us -> 178 us
  blocking collectives: 223 us -> 394 us
  starting transfers between devices: 38 us -> 83.7 us
  local copies, waits for them, and re-layouts: 46.9 us -> 57.7 us
    all_gather x1 -> x0, waiting for transfers between devices: 228 us -> none  [on_device(): weight_out = lax.all_gather(expert_out, 'blk', axis=1, tiled=True)[0]]
    all_gather x2, blocking collectives: 223 us -> 394 us  [combined_all(): gathered = jax.tree.map(lambda a: lax.all_gather(a, axis), part)]
    all_gather x1, waiting for transfers between devices: 228 us -> 146 us  [on_device(): weight_in = lax.all_gather(expert_in, 'blk', axis=1, tiled=True)[0]]
    all_to_all x1, starting transfers between devices: 3.98 us -> 39.7 us  [on_device(): lax.all_to_all(dispatch, 'expert', split_axis=0, concat_axis=0, tiled=True)]
    all_gather x1, waiting for transfers between devices: 32.4 us -> 0.02 us  [on_device(): lax.all_gather(out_weight, 'expert', axis=0, tiled=True)]
    all_to_all x0 -> x1, starting transfers between devices: none -> 16 us  [on_device(): lax.all_to_all(jnp.stack([load for _ in range(lax.axis_size(link_axis))],...]
    all_gather x1, waiting for transfers between devices: 9.65 us -> 0.02 us  [combined_all(): gathered = jax.tree.map(lambda a: lax.all_gather(a, axis), part)]
  transfers between devices with their start and end apart: 6 -> 6, of which waited for: 5 -> 2; matrix products, arithmetic and copies ran while one was open for 10% -> 12% of each run, Pallas kernels for 0% -> 0%
where the time goes in v1:
time: 787 us; the launch traced here: 785 us
  blocking collectives  394 us (50%)
  waiting for transfers between devices  178 us (23%)
  starting transfers between devices  83.7 us (11%)
  local copies, waits for them, and re-layouts  57.7 us (7%)
  other arithmetic  38.4 us (5%)
  matrix products  17.2 us (2%)
  between operations  14.3 us (2%)
    all_gather x2, blocking collectives, combined_all(): gathered = jax.tree.map(lambda a: lax.all_gather(a, axis), part)  394 us
    all_gather x1, waiting for transfers between devices, on_device(): weight_in = lax.all_gather(expert_in, 'blk', axis=1, tiled=True)[0]  146 us
    all_to_all x1, starting transfers between devices, on_device(): lax.all_to_all(dispatch, 'expert', split_axis=0, concat_axis=0, tiled=True)  39.7 us
    add x31, other arithmetic, pair_join(): output = expand(former_scale, former[2]) + expand(latter_scale, latter[2])  33.7 us
    all_to_all x1, waiting for transfers between devices, on_device(): lax.all_to_all(expert_y, 'expert', split_axis=0, concat_axis=0, tiled=True)  30 us
    all_to_all x1, starting transfers between devices, on_device(): lax.all_to_all(expert_y, 'expert', split_axis=0, concat_axis=0, tiled=True)  27.9 us
    mul x127, local copies, waits for them, and re-layouts, expand(): return (shaped * factor[..., None]).reshape(output.shape)  21.2 us
    all_to_all x1, starting transfers between devices, on_device(): lax.all_to_all(jnp.stack([load for _ in range(lax.axis_size(link_axis))],...  16 us
  transfers between devices with their start and end apart: 6, of which 2 were waited for; matrix products, arithmetic and copies ran while one was open for 12% of the time, Pallas kernels for 0%

profile of v1, /device:TPU:1, one launch (start us, length us, event | category | flops | bytes accessed | tf_op | source)
XLA Modules:
  0.0 785.1 jit_solution(8370357748117925641)
XLA Ops:
  7.2 1.1 fusion.59
  8.5 1.2 copy.101
  12.7 2.0 stack.2
  14.8 16.0 %all-to-all-start.1 = ((bf16[32,1,44,1024]{3,2,1,0:T(8,128)(2,1)}), bf16[32,1,44,1024]{3,2,1,0:T(8,128)(2,1)}, u32[]{:S(2)}, u32[]{:S(2)}) async-start(bf16[32,1,44,1024]{3,2,1,0:T(8,128)(2,1)} %stack.2), calls=%async_computation.1 | async-start | bytes 6291456 | tf_op jit(solution)/shard_map/all_to_all | solution.py:153
  32.0 292.8 %all-gather = f32[64,64,8]{1,2,0:T(8,128)S(1)} all-gather(f32[2,64,8]{1,2,0:T(8,128)S(1)} %get-tuple-element.216), channel_id=2, replica_groups=mesh['blk'=32,'expert'=16] {'blk'}, dimensions={0}, use_global_device_ids=true | all-gather | bytes 135168 | tf_op jit(solution)/shard_map/all_gather | solution.py:11
  325.5 101.3 %all-gather.1 = f32[64,64,8]{1,2,0:T(8,128)S(1)} all-gather(f32[2,64,8]{1,2,0:T(8,128)S(1)} %convert_reduce_fusion), channel_id=3, replica_groups=mesh['blk'=32,'expert'=16] {'blk'}, dimensions={0}, use_global_device_ids=true | all-gather | bytes 135168 | tf_op jit(solution)/shard_map/all_gather | solution.py:11
  428.2 1.1 copy.94
  436.4 62.7 %while.19 = (s32[]{:T(128)}, f32[2,64,8]{1,2,0:T(8,128)S(1)}, f32[2,64,8]{1,2,0:T(8,128)S(1)}, f32[2,64,512]{2,1,0:T(8,128)S(1)}, f32[32,2,64,8]{2,3,1,0:T(8,128...) while((s32[]{:T(128)}, f32[2,64,8]{1,2,0:T(8,128)S(1)}, ...), condition=%wide.region_7.8_spmd, body=%wide.region_6.7_spmd.sunk | while | flops 202757 | bytes 2941079 | solution.py:16
  437.3 1.1 fusion.79
  439.3 1.1 fusion.79
  441.4 1.1 fusion.79
  443.4 1.1 fusion.79
  445.4 1.1 fusion.79
  447.4 1.1 fusion.79
  449.4 1.1 fusion.79
  451.5 1.1 fusion.79
  453.5 1.1 fusion.79
  455.5 1.1 fusion.79
  457.5 1.1 fusion.79
  459.6 1.1 fusion.79
  461.6 1.1 fusion.79
  463.6 1.1 fusion.79
  465.6 1.1 fusion.79
  467.7 1.1 fusion.79
  469.7 1.1 fusion.79
  471.7 1.1 fusion.79
  473.7 1.1 fusion.79
  475.8 1.1 fusion.79
  477.8 1.1 fusion.79
  479.8 1.1 fusion.79
  481.8 1.1 fusion.79
  483.8 1.1 fusion.79
  485.9 1.1 fusion.79
  487.9 1.1 fusion.79
  491.9 1.1 fusion.79
  498.0 1.1 fusion.79
  500.1 1.7 multiply_reduce_fusion
  503.6 1.1 reshape.238
  504.7 39.7 %all-to-all-start = ((bf16[16,21,1024]{2,1,0:T(8,128)(2,1)}), bf16[16,21,1024]{2,1,0:T(8,128)(2,1)S(1)}, u32[]{:S(2)}, u32[]{:S(2)}) async-start(bf16[16,21,1024]{2,1,0:T(8,128)(2,1)} %reshape.238), calls=%async_computation | async-start | bytes 1572864 | tf_op jit(solution)/shard_map/all_to_all | solution.py:149
  544.5 146.4 %all-gather.10.cloned.1.call-done = bf16[1,1408,2,1024]{3,2,0,1:T(2,128)(2,1)} async-done(((bf16[1,44,2,1024]{3,2,0,1:T(2,128)(2,1)}), bf16[1,1408,2,1024]{3,2,0,1:T(2,128)(2,1)}) %all-gather.10.cloned.1.call-update) | async-done | bytes 5767184 | tf_op jit(solution)/shard_map/all_gather | solution.py:151
  690.9 6.9 copy.149
  697.8 5.2 squeeze_reshape.3
  703.0 1.1 reshape.239
  704.1 5.1 fusion.11
  709.2 5.8 convolution_convert_fusion
  715.0 2.2 reshape.240
  717.2 27.9 %all-to-all-start.2 = ((bf16[16,21,1024]{2,1,0:T(8,128)(2,1)}), bf16[16,21,1024]{2,1,0:T(8,128)(2,1)S(1)}, u32[]{:S(2)}, u32[]{:S(2)}) async-start(bf16[16,21,1024]{2,1,0:T(8,128)(2,1)} %reshape.240), calls=%async_computation.2 | async-start | bytes 1572864 | tf_op jit(solution)/shard_map/all_to_all | solution.py:168
  745.7 30.0 %all-to-all-done.2 = bf16[16,21,1024]{2,1,0:T(8,128)(2,1)S(1)} async-done(((bf16[16,21,1024]{2,1,0:T(8,128)(2,1)}), bf16[16,21,1024]{2,1,0:T(8,128)(2,1)S(1)}, u32[]{:S(2)}, u32[]{:S(2)}) %all-to-all-start.2) | async-done | bytes 688160 | tf_op jit(solution)/shard_map/all_to_all | solution.py:168
  (339 shorter events, 49.8 us)
Async XLA Ops:
  7.2 738.3 %copy-start = (bf16[1024,16]{0,1:T(8,128)(2,1)S(1)}, bf16[1024,16]{0,1:T(8,128)(2,1)}, u32[]{:S(2)}) copy-start(bf16[1024,16]{0,1:T(8,128)(2,1)} %param.34) | copy-start | bytes 98308
  7.2 2.6 copy-start.5
  7.2 428.2 %all-gather.6.cloned.1.call-start = ((), (), s32[]{:S(2)}) async-start(), calls=%async_computation.3 | async-start | bytes 8650752 | tf_op jit(solution)/shard_map/all_gather | solution.py:11
  10.4 2.3 copy-start.9
  12.0 488.1 %all-gather.8.cloned.1.call-start = ((), (), s32[]{:S(2)}) async-start(), calls=%async_computation.4 | async-start | bytes 1114112 | tf_op jit(solution)/shard_map/all_gather | solution.py:123
  14.8 490.0 %all-to-all-start.1 = ((bf16[32,1,44,1024]{3,2,1,0:T(8,128)(2,1)}), bf16[32,1,44,1024]{3,2,1,0:T(8,128)(2,1)}, u32[]{:S(2)}, u32[]{:S(2)}) async-start(bf16[32,1,44,1024]{3,2,1,0:T(8,128)(2,1)} %stack.2), calls=%async_computation.1 | async-start | bytes 6291456 | tf_op jit(solution)/shard_map/all_to_all | solution.py:153
  30.8 396.4 %copy-start.6 = (bf16[2,64,3,512]{3,1,2,0:T(8,128)(2,1)S(1)}, bf16[2,64,3,512]{3,1,2,0:T(8,128)(2,1)}, u32[]{:S(2)}) copy-start(bf16[2,64,3,512]{3,1,2,0:T(8,128)(2,1)} %param.20) | copy-start | bytes 1179652
  30.8 660.1 %all-gather.10.cloned.1.call-start = ((), (), s32[]{:S(2)}) async-start(), calls=%async_computation.5 | async-start | bytes 5947392 | tf_op jit(solution)/shard_map/all_gather | solution.py:151
  31.9 395.7 %copy-start.10 = (s32[2,64,64]{2,1,0:T(8,128)S(1)}, s32[2,64,64]{2,1,0:T(8,128)}, u32[]{:S(2)}) copy-start(s32[2,64,64]{2,1,0:T(8,128)} %param.21) | copy-start | bytes 98308
  32.0 395.8 %copy-start.8 = (bf16[2,128,512]{2,1,0:T(8,128)(2,1)S(1)}, bf16[2,128,512]{2,1,0:T(8,128)(2,1)}, u32[]{:S(2)}) copy-start(bf16[2,128,512]{2,1,0:T(8,128)(2,1)} %param.22) | copy-start | bytes 786436
  324.7 103.2 %copy-start.15 = (s32[2]{0:T(128)S(1)}, s32[2]{0:T(128)}, u32[]{:S(2)}) copy-start(s32[2]{0:T(128)} %param.24) | copy-start | bytes 28
  430.9 0.9 copy-start.12
  430.9 0.9 copy-start.13
  430.9 0.9 copy-start.11
  436.4 63.7 %copy-start.7 = (bf16[128,1024]{1,0:T(8,128)(2,1)S(1)}, bf16[128,1024]{1,0:T(8,128)(2,1)}, u32[]{:S(2)}) copy-start(bf16[128,1024]{1,0:T(8,128)(2,1)} %param.25) | copy-start | bytes 786436
  501.9 0.7 copy-start.2
  504.7 198.3 %all-to-all-start = ((bf16[16,21,1024]{2,1,0:T(8,128)(2,1)}), bf16[16,21,1024]{2,1,0:T(8,128)(2,1)S(1)}, u32[]{:S(2)}, u32[]{:S(2)}) async-start(bf16[16,21,1024]{2,1,0:T(8,128)(2,1)} %reshape.238), calls=%async_computation | async-start | bytes 1572864 | tf_op jit(solution)/shard_map/all_to_all | solution.py:149
  704.1 5.1 copy-start.1
  715.0 30.4 %copy-start.14 = (s32[2,8]{1,0:T(2,128)S(1)}, s32[2,8]{1,0:T(2,128)}, u32[]{:S(2)}) copy-start(s32[2,8]{1,0:T(2,128)} %param.26) | copy-start | bytes 196
  715.0 30.5 %copy-start.3 = (bf16[132,1024]{1,0:T(8,128)(2,1)S(1)}, bf16[132,1024]{1,0:T(8,128)(2,1)}, u32[]{:S(2)}) copy-start(bf16[132,1024]{1,0:T(8,128)(2,1)} %copy-done.2) | copy-start | bytes 811012
  717.2 58.5 %all-to-all-start.2 = ((bf16[16,21,1024]{2,1,0:T(8,128)(2,1)}), bf16[16,21,1024]{2,1,0:T(8,128)(2,1)S(1)}, u32[]{:S(2)}, u32[]{:S(2)}) async-start(bf16[16,21,1024]{2,1,0:T(8,128)(2,1)} %reshape.240), calls=%async_computation.2 | async-start | bytes 1572864 | tf_op jit(solution)/shard_map/all_to_all | solution.py:168
  776.5 2.1 copy-start.4
Sparse Core Ops, SparseCore 0:
  12.1 352.3 all-gather.5
  367.8 88.7 all-gather.7
  458.7 232.1 all-gather.9
